TPU v7x, 256 devices: a whole 4x4x8 slice. The times are simulated.
256 devices in a mesh: tm: 16 (over y_lo, x, core), blk: 8 (over z), samp: 2 (over y_hi).
Axes of the slice: x: 4, y: 4 (y_hi: 2, y_lo: 2; y = y_hi * 2 + y_lo), z: 8, core: 2. Of those that a mesh axis runs over, the one named last changes fastest.
Arguments:
- prior_path: float32 [32, 16, 1024], P('tm', 'samp', 'blk'), may hold values from -6 to 6
- observed: float32 [32, 256], P('tm', 'blk'), may hold values from -6 to 6
- obs_mask: int32 [32, 32], P('tm', 'blk'), may hold values 0 or 1
- noise_draw: float32 [32, 16, 256], P('tm', 'samp', 'blk'), may hold values from -6 to 6
- wend_blocks: float32 [128, 8, 8], P('blk'), may hold values from -1 to 1
- block_cols: int32 [128], P('blk'), may hold values from 0 to 31, as said below
- start_mean: float32 [16, 1024], P('samp', 'blk'), may hold values from -6 to 6
- trans_mats: bfloat16 [32, 1024, 1024], P('tm', 'blk', 'samp')
- gain_mats: bfloat16 [32, 1024, 256], P('tm', 'blk', 'samp'), may hold values from -0.375 to 0.375
- smooth_mats: bfloat16 [32, 1024, 1024], P('tm', 'blk', 'samp')
- site_trans: float32 [4, 4], replicated, may hold values from -2.5 to 2.5
Outputs:
- posterior_path: float32 [32, 16, 1024], P('tm', 'samp', 'blk')
Inputs may be any that keep to these rules, and one draw needn't show every extreme that they name: `block_cols`: entry 4 i names block i itself, entries 4 i + 1 to 4 i + 3 name three different blocks among i - 2, i - 1, i + 1, i + 2 taken modulo 32.
All inputs are finite; a program needn't handle non-finite values. No bound on the sum of `obs_mask` on one device may be relied on, other than what follows from the above.
Results may differ from a plain program's by a relative error of at most 0.0003.
Values may be sent and summed in bfloat16 or wider, within the bound.
No kernel may reach another device: no remote copies, remote signals or barrier semaphores. Data moves between devices by JAX's collectives and lax.ppermute only.
A program may use at most 64 MiB of HBM per device.

v0:
```python
import jax
import jax.numpy as jnp
from jax import lax
from jax.sharding import PartitionSpec as P

highest = lax.Precision.HIGHEST


def with_halo(value, sides, width):
    for axis, dim in sides:
        count, length = (lax.axis_size(axis), value.shape[dim])
        up = [(i, (i + 1) % count) for i in range(count)]
        down = [(j, i) for i, j in up]
        last = lax.slice_in_dim(value, length - width, length, axis=dim)
        initial = lax.slice_in_dim(value, 0, width, axis=dim)
        before = lax.ppermute(last, axis, up)
        after = lax.ppermute(initial, axis, down)
        value = jnp.concatenate([before, value, after], axis=dim)
    return value


def shifted(value, axis, steps):
    count = lax.axis_size(axis)
    initial, last = (max(0, -steps), min(count, count - steps))
    return lax.ppermute(value, axis, [(source, source + steps) for source in range(initial, last)])


def apply_rows(matrix, states):
    return jnp.einsum("ij,sj->si", matrix, states, precision=highest)


def on_device(
    prior_path,
    observed,
    obs_mask,
    noise_draw,
    wend_blocks,
    block_cols,
    start_mean,
    trans_mats,
    gain_mats,
    smooth_mats,
    site_trans,
):
    trans_mats, gain_mats, smooth_mats = (
        lax.all_gather(trans_mats, "samp", axis=2, tiled=True),
        lax.all_gather(gain_mats, "samp", axis=2, tiled=True),
        lax.all_gather(smooth_mats, "samp", axis=2, tiled=True),
    )
    step_count, sample_count, local_sites = noise_draw.shape
    block_sites = wend_blocks.shape[1]
    local_blocks = local_sites // block_sites
    cycle_size = lax.axis_size("blk")
    block_count = local_blocks * cycle_size
    row_count = trans_mats.shape[1]
    state_count = row_count * cycle_size
    widened = with_halo(noise_draw, (("blk", 2),), 2 * block_sites)
    rim_blocks = widened.reshape(step_count, sample_count, local_blocks + 4, block_sites)
    pair_rows = jnp.arange(local_blocks * 4, dtype=jnp.int32) // 4
    first_block = lax.axis_index("blk") * local_blocks
    offset = (block_cols - first_block - pair_rows + 2) % block_count
    position = pair_rows + offset
    chooser = (position[:, None] == jnp.arange(local_blocks + 4, dtype=jnp.int32)[None, :]).astype(
        jnp.float32
    )
    picked = jnp.einsum("pl,tslj->tspj", chooser, rim_blocks, precision=highest)
    mixed = jnp.einsum("tspj,pij->tspi", picked, wend_blocks, precision=highest)
    obs_noise = jnp.sum(
        mixed.reshape(step_count, sample_count, local_blocks, 4, block_sites), axis=3
    ).reshape(step_count, sample_count, local_sites)
    first_comp = prior_path.reshape(step_count, sample_count, local_sites, 4)[:, :, :, 0]
    seen_mask = jnp.repeat(obs_mask.astype(jnp.float32), block_sites, axis=1)
    residual = seen_mask[:, None, :] * (observed[:, None, :] - first_comp - obs_noise)
    all_resid = lax.all_gather(residual, "blk", axis=2, tiled=True)
    inputs = jnp.einsum("tij,tsj->tsi", gain_mats, all_resid, precision=highest)
    left_trans = trans_mats[1]
    left_smooth = smooth_mats[0]
    forward_pair = jnp.dot(
        left_trans,
        lax.all_gather(trans_mats[0], "blk", axis=0, tiled=True),
        preferred_element_type=jnp.float32,
    )
    backward_pair = jnp.dot(
        left_smooth,
        lax.all_gather(smooth_mats[1], "blk", axis=0, tiled=True),
        preferred_element_type=jnp.float32,
    )
    first_input, initial = (
        lax.all_gather(inputs[0], "blk", axis=1, tiled=True),
        lax.all_gather(start_mean, "blk", axis=1, tiled=True),
    )
    carry_input = apply_rows(trans_mats[1], first_input) + inputs[1]
    is_first = lax.axis_index("tm") == 0
    time_size = lax.axis_size("tm")
    level_count = (time_size - 1).bit_length()
    matrix, vector = shifted((forward_pair, carry_input), "tm", 1)
    vector = jnp.where(is_first, start_mean, vector)
    for level in range(level_count):
        received_m, received_v = shifted((matrix, vector), "tm", 1 << level)
        complete_m, complete_v = (
            lax.all_gather(received_m, "blk", axis=0, tiled=True),
            lax.all_gather(received_v, "blk", axis=1, tiled=True),
        )
        matrix, vector = (
            jnp.dot(matrix, complete_m, precision=highest),
            apply_rows(matrix, complete_v) + vector,
        )
    entry_state = lax.all_gather(vector, "blk", axis=1, tiled=True)
    filtered = jnp.stack(
        [
            apply_rows(trans_mats[0], entry_state) + inputs[0],
            apply_rows(forward_pair, entry_state) + carry_input,
        ]
    )
    site_kron = jnp.kron(jnp.eye(row_count // 4, dtype=jnp.float32), site_trans)
    predicted = jnp.einsum("ij,tsj->tsi", site_kron, filtered, precision=highest)
    all_pred = lax.all_gather(predicted, "blk", axis=2, tiled=True)
    offsets = filtered - jnp.einsum("tij,tsj->tsi", smooth_mats, all_pred, precision=highest)
    is_last = lax.axis_index("tm") == time_size - 1
    late_offset = jnp.where(is_last, filtered[1], offsets[1])
    all_late = lax.all_gather(late_offset, "blk", axis=1, tiled=True)
    back_offset = apply_rows(smooth_mats[0], all_late) + offsets[0]

    def relay_back(relay_turn, later_now):
        emitted = apply_rows(backward_pair, later_now) + back_offset
        complete = lax.all_gather(emitted, "blk", axis=1, tiled=True)
        received = shifted(complete, "tm", -1)
        return jnp.where(lax.axis_index("tm") == time_size - 2 - relay_turn, received, later_now)

    later_state = lax.fori_loop(
        0, time_size - 1, relay_back, jnp.zeros((sample_count, state_count), jnp.float32)
    )
    smoothed = jnp.stack(
        [
            apply_rows(backward_pair, later_state) + back_offset,
            apply_rows(smooth_mats[1], later_state) + late_offset,
        ]
    )
    return prior_path + smoothed


def solution(mesh):
    placed = (
        P("tm", "samp", "blk"),
        P("tm", "blk"),
        P("tm", "blk"),
        P("tm", "samp", "blk"),
        P("blk", None, None),
        P("blk"),
        P("samp", "blk"),
        P("tm", "blk", "samp"),
        P("tm", "blk", "samp"),
        P("tm", "blk", "samp"),
        P(),
    )
    return jax.shard_map(
        on_device, mesh=mesh, in_specs=placed, out_specs=P("tm", "samp", "blk"), check_vma=False
    )
```

profile of v0, /device:TPU:7, one launch (start us, length us, event | category | flops | bytes accessed | tf_op | source)
XLA Modules:
  0.0 952.8 jit_solution(16144380244082695753)
XLA Ops:
  6.5 9.6 %all_gather.63 = bf16[2,128,1024]{2,1,0:T(8,128)(2,1)S(1)} all-gather(bf16[2,128,512]{2,1,0:T(8,128)(2,1)} %param.20), channel_id=1, replica_groups=mesh['tm'=16,'blk'=8,'samp'=2] {'samp'}, dimensions={2}, use_global_device_ids=true | all-gather | bytes 786432 | tf_op jit(solution)/shard_map/all_gather | solution.py:46
  16.9 41.3 %all-gather.17.cloned.1.call-done = bf16[1,1024,1024]{2,1,0:T(8,128)(2,1)} async-done(((bf16[1,128,1024]{2,1,0:T(8,128)(2,1)}), bf16[1,1024,1024]{2,1,0:T(8,128)(2,1)}) %all-gather.17.cloned.1.call-update) | async-done | bytes 2097168 | tf_op jit(solution)/shard_map/all_gather | solution.py:80
  87.2 53.6 %all-gather.9.cloned.1.call-done = f32[1024,1024]{1,0:T(8,128)} async-done(((f32[128,1024]{1,0:T(8,128)}), f32[1024,1024]{1,0:T(8,128)}) %all-gather.9.cloned.1.call-update) | async-done | bytes 4194320 | tf_op jit(solution)/shard_map/all_gather | solution.py:101
  148.7 11.6 %collective-permute-done.9 = f32[128,1024]{1,0:T(8,128)S(1)} collective-permute-done((f32[128,1024]{1,0:T(8,128)S(1)}, f32[128,1024]{1,0:T(8,128)S(1)}, u32[]{:S(2)}, u32[]{:S(2)}) %collective-permute-start.9) | collective-permute-done | bytes 524320 | tf_op jit(solution)/shard_map/ppermute | solution.py:25
  161.2 8.4 all_gather.58
  170.5 45.1 %all-gather.11.cloned.1.call-done = f32[1024,1024]{1,0:T(8,128)} async-done(((f32[128,1024]{1,0:T(8,128)}), f32[1024,1024]{1,0:T(8,128)}) %all-gather.11.cloned.1.call-update) | async-done | bytes 4194320 | tf_op jit(solution)/shard_map/all_gather | solution.py:101
  224.2 12.2 %collective-permute-done.11 = f32[128,1024]{1,0:T(8,128)S(1)} collective-permute-done((f32[128,1024]{1,0:T(8,128)S(1)}, f32[128,1024]{1,0:T(8,128)S(1)}, u32[]{:S(2)}, u32[]{:S(2)}) %collective-permute-start.11) | collective-permute-done | bytes 524320 | tf_op jit(solution)/shard_map/ppermute | solution.py:25
  246.9 19.8 %all_gather.60 = f32[2,8,256]{1,0,2:T(2,128)S(1)} all-gather(f32[2,8,32]{1,0,2:T(2,128)S(1)} %copy.27), channel_id=1, replica_groups=mesh['tm'=16,'blk'=8,'samp'=2] {'blk'}, dimensions={2}, use_global_device_ids=true | all-gather | bytes 18432 | tf_op jit(solution)/shard_map/all_gather | solution.py:74
  267.0 20.3 %all-gather.1 = f32[1,8,1024]{2,1,0:T(8,128)S(1)} all-gather(f32[1,8,128]{2,1,0:T(8,128)S(1)} %slice.52), channel_id=3, replica_groups=mesh['tm'=16,'blk'=8,'samp'=2] {'blk'}, dimensions={2}, use_global_device_ids=true | all-gather | bytes 36864 | tf_op jit(solution)/shard_map/all_gather | solution.py:89
  287.5 16.8 %collective-permute-start.3 = (f32[8,128]{1,0:T(8,128)S(1)}, f32[8,128]{1,0:T(8,128)S(1)}, u32[]{:S(2)}, u32[]{:S(2)}) collective-permute-start(f32[8,128]{1,0:T(8,128)S(1)} %convolution_add_fusion.4), channel_id=1, source_target_pairs={{0,16},{16,32},{32,48},{48,64},{64,80},{80,96},{96,112},{112,128},... | collective-permute-start | bytes 12296 | tf_op jit(solution)/shard_map/ppermute | solution.py:25
  312.1 18.1 %all_gather.64 = f32[8,1024]{1,0:T(8,128)S(1)} all-gather(f32[8,128]{1,0:T(8,128)S(1)} %collective-permute-done.4), channel_id=1, replica_groups=mesh['tm'=16,'blk'=8,'samp'=2] {'blk'}, dimensions={1}, use_global_device_ids=true | all-gather | bytes 36864 | tf_op jit(solution)/shard_map/all_gather | solution.py:102
  335.1 18.1 %all_gather.66 = f32[8,1024]{1,0:T(8,128)S(1)} all-gather(f32[8,128]{1,0:T(8,128)S(1)} %collective-permute-done.6), channel_id=1, replica_groups=mesh['tm'=16,'blk'=8,'samp'=2] {'blk'}, dimensions={1}, use_global_device_ids=true | all-gather | bytes 36864 | tf_op jit(solution)/shard_map/all_gather | solution.py:102
  359.5 18.3 %all_gather.68 = f32[8,1024]{1,0:T(8,128)S(1)} all-gather(f32[8,128]{1,0:T(8,128)S(1)} %collective-permute-done.8), channel_id=1, replica_groups=mesh['tm'=16,'blk'=8,'samp'=2] {'blk'}, dimensions={1}, use_global_device_ids=true | all-gather | bytes 36864 | tf_op jit(solution)/shard_map/all_gather | solution.py:102
  381.8 18.1 %all_gather.70 = f32[8,1024]{1,0:T(8,128)S(1)} all-gather(f32[8,128]{1,0:T(8,128)S(1)} %collective-permute-done.10), channel_id=1, replica_groups=mesh['tm'=16,'blk'=8,'samp'=2] {'blk'}, dimensions={1}, use_global_device_ids=true | all-gather | bytes 36864 | tf_op jit(solution)/shard_map/all_gather | solution.py:102
  405.0 18.2 %all_gather.72 = f32[8,1024]{1,0:T(8,128)S(1)} all-gather(f32[8,128]{1,0:T(8,128)S(1)} %convolution_add_fusion.7), channel_id=1, replica_groups=mesh['tm'=16,'blk'=8,'samp'=2] {'blk'}, dimensions={1}, use_global_device_ids=true | all-gather | bytes 36864 | tf_op jit(solution)/shard_map/all_gather | solution.py:108
  424.2 18.2 %all_gather.73 = f32[2,8,1024]{2,1,0:T(8,128)S(1)} all-gather(f32[2,8,128]{2,1,0:T(8,128)S(1)} %fusion.18), channel_id=1, replica_groups=mesh['tm'=16,'blk'=8,'samp'=2] {'blk'}, dimensions={2}, use_global_device_ids=true | all-gather | bytes 73728 | tf_op jit(solution)/shard_map/all_gather | solution.py:117
  442.9 18.1 %all_gather.74 = f32[8,1024]{1,0:T(8,128)S(1)} all-gather(f32[8,128]{1,0:T(8,128)S(1)} %fusion.19), channel_id=1, replica_groups=mesh['tm'=16,'blk'=8,'samp'=2] {'blk'}, dimensions={1}, use_global_device_ids=true | all-gather | bytes 36864 | tf_op jit(solution)/shard_map/all_gather | solution.py:121
  461.3 483.5 %while.14 = (s32[]{:T(128)}, f32[8,1024]{1,0:T(8,128)S(1)}, f32[128,1024]{1,0:T(8,128)S(1)}, f32[8,128]{1,0:T(8,128)S(1)}, s32[]{:T(128)}, /*index=5*/s32[]{:T(128)}, u32[]{:T(128)}, u32[]{:T(128)}, s32[]{:T(128)}) while((s32[]{:T(128)}, f32[8,1024]{1,0:T(8,128)S(1)}, f32[128,1024]{1,0:T(8,128)S(1)}, f32[8,128]{1,0:T(8,128)S(1)}, ...), condition=%wide.region_2.3_spmd.clone, body=%wide.region_1.2_spmd.clone.sunk | while | flops 12608520 | bytes 831686 | solution.py:130
  461.8 18.2 %all_gather.77 = f32[8,1024]{1,0:T(8,128)S(1)} all-gather(f32[8,128]{1,0:T(8,128)S(1)} %convolution_add_fusion.12), channel_id=1, replica_groups=mesh['tm'=16,'blk'=8,'samp'=2] {'blk'}, dimensions={1}, use_global_device_ids=true | all-gather | bytes 36864 | tf_op jit(solution)/shard_map/while/body/eval_jaxpr/all_gather | solution.py:126
  480.0 57.5 %collective-permute-start = (f32[8,1024]{1,0:T(8,128)S(1)}, f32[8,1024]{1,0:T(8,128)S(1)}, u32[]{:S(2)}, u32[]{:S(2)}) collective-permute-start(f32[8,1024]{1,0:T(8,128)S(1)} %all_gather.77), channel_id=1, source_target_pairs={{16,0},{32,16},{48,32},{64,48},{80,64},{96,80},{112,96},{128,112},... | collective-permute-start | bytes 98312 | tf_op jit(solution)/shard_map/while/body/eval_jaxpr/ppermute | solution.py:25
  537.5 8.6 collective-permute-done
  546.5 18.2 %all_gather.77 = f32[8,1024]{1,0:T(8,128)S(1)} all-gather(f32[8,128]{1,0:T(8,128)S(1)} %convolution_add_fusion.12), channel_id=1, replica_groups=mesh['tm'=16,'blk'=8,'samp'=2] {'blk'}, dimensions={1}, use_global_device_ids=true | all-gather | bytes 36864 | tf_op jit(solution)/shard_map/while/body/eval_jaxpr/all_gather | solution.py:126
  566.6 7.9 collective-permute-done
  575.0 18.2 %all_gather.77 = f32[8,1024]{1,0:T(8,128)S(1)} all-gather(f32[8,128]{1,0:T(8,128)S(1)} %convolution_add_fusion.12), channel_id=1, replica_groups=mesh['tm'=16,'blk'=8,'samp'=2] {'blk'}, dimensions={1}, use_global_device_ids=true | all-gather | bytes 36864 | tf_op jit(solution)/shard_map/while/body/eval_jaxpr/all_gather | solution.py:126
  595.1 7.9 collective-permute-done
  603.4 18.2 %all_gather.77 = f32[8,1024]{1,0:T(8,128)S(1)} all-gather(f32[8,128]{1,0:T(8,128)S(1)} %convolution_add_fusion.12), channel_id=1, replica_groups=mesh['tm'=16,'blk'=8,'samp'=2] {'blk'}, dimensions={1}, use_global_device_ids=true | all-gather | bytes 36864 | tf_op jit(solution)/shard_map/while/body/eval_jaxpr/all_gather | solution.py:126
  623.5 7.9 collective-permute-done
  631.9 18.2 %all_gather.77 = f32[8,1024]{1,0:T(8,128)S(1)} all-gather(f32[8,128]{1,0:T(8,128)S(1)} %convolution_add_fusion.12), channel_id=1, replica_groups=mesh['tm'=16,'blk'=8,'samp'=2] {'blk'}, dimensions={1}, use_global_device_ids=true | all-gather | bytes 36864 | tf_op jit(solution)/shard_map/while/body/eval_jaxpr/all_gather | solution.py:126
  652.0 7.9 collective-permute-done
  660.4 18.2 %all_gather.77 = f32[8,1024]{1,0:T(8,128)S(1)} all-gather(f32[8,128]{1,0:T(8,128)S(1)} %convolution_add_fusion.12), channel_id=1, replica_groups=mesh['tm'=16,'blk'=8,'samp'=2] {'blk'}, dimensions={1}, use_global_device_ids=true | all-gather | bytes 36864 | tf_op jit(solution)/shard_map/while/body/eval_jaxpr/all_gather | solution.py:126
  680.5 7.9 collective-permute-done
  688.9 18.2 %all_gather.77 = f32[8,1024]{1,0:T(8,128)S(1)} all-gather(f32[8,128]{1,0:T(8,128)S(1)} %convolution_add_fusion.12), channel_id=1, replica_groups=mesh['tm'=16,'blk'=8,'samp'=2] {'blk'}, dimensions={1}, use_global_device_ids=true | all-gather | bytes 36864 | tf_op jit(solution)/shard_map/while/body/eval_jaxpr/all_gather | solution.py:126
  709.0 7.9 collective-permute-done
  717.4 18.2 %all_gather.77 = f32[8,1024]{1,0:T(8,128)S(1)} all-gather(f32[8,128]{1,0:T(8,128)S(1)} %convolution_add_fusion.12), channel_id=1, replica_groups=mesh['tm'=16,'blk'=8,'samp'=2] {'blk'}, dimensions={1}, use_global_device_ids=true | all-gather | bytes 36864 | tf_op jit(solution)/shard_map/while/body/eval_jaxpr/all_gather | solution.py:126
  737.5 7.9 collective-permute-done
  745.9 18.2 %all_gather.77 = f32[8,1024]{1,0:T(8,128)S(1)} all-gather(f32[8,128]{1,0:T(8,128)S(1)} %convolution_add_fusion.12), channel_id=1, replica_groups=mesh['tm'=16,'blk'=8,'samp'=2] {'blk'}, dimensions={1}, use_global_device_ids=true | all-gather | bytes 36864 | tf_op jit(solution)/shard_map/while/body/eval_jaxpr/all_gather | solution.py:126
  766.0 7.9 collective-permute-done
  774.3 18.2 %all_gather.77 = f32[8,1024]{1,0:T(8,128)S(1)} all-gather(f32[8,128]{1,0:T(8,128)S(1)} %convolution_add_fusion.12), channel_id=1, replica_groups=mesh['tm'=16,'blk'=8,'samp'=2] {'blk'}, dimensions={1}, use_global_device_ids=true | all-gather | bytes 36864 | tf_op jit(solution)/shard_map/while/body/eval_jaxpr/all_gather | solution.py:126
  794.5 7.9 collective-permute-done
  802.8 18.2 %all_gather.77 = f32[8,1024]{1,0:T(8,128)S(1)} all-gather(f32[8,128]{1,0:T(8,128)S(1)} %convolution_add_fusion.12), channel_id=1, replica_groups=mesh['tm'=16,'blk'=8,'samp'=2] {'blk'}, dimensions={1}, use_global_device_ids=true | all-gather | bytes 36864 | tf_op jit(solution)/shard_map/while/body/eval_jaxpr/all_gather | solution.py:126
  822.9 7.9 collective-permute-done
  831.3 18.2 %all_gather.77 = f32[8,1024]{1,0:T(8,128)S(1)} all-gather(f32[8,128]{1,0:T(8,128)S(1)} %convolution_add_fusion.12), channel_id=1, replica_groups=mesh['tm'=16,'blk'=8,'samp'=2] {'blk'}, dimensions={1}, use_global_device_ids=true | all-gather | bytes 36864 | tf_op jit(solution)/shard_map/while/body/eval_jaxpr/all_gather | solution.py:126
  851.4 7.9 collective-permute-done
  859.8 18.2 %all_gather.77 = f32[8,1024]{1,0:T(8,128)S(1)} all-gather(f32[8,128]{1,0:T(8,128)S(1)} %convolution_add_fusion.12), channel_id=1, replica_groups=mesh['tm'=16,'blk'=8,'samp'=2] {'blk'}, dimensions={1}, use_global_device_ids=true | all-gather | bytes 36864 | tf_op jit(solution)/shard_map/while/body/eval_jaxpr/all_gather | solution.py:126
  888.3 18.2 %all_gather.77 = f32[8,1024]{1,0:T(8,128)S(1)} all-gather(f32[8,128]{1,0:T(8,128)S(1)} %convolution_add_fusion.12), channel_id=1, replica_groups=mesh['tm'=16,'blk'=8,'samp'=2] {'blk'}, dimensions={1}, use_global_device_ids=true | all-gather | bytes 36864 | tf_op jit(solution)/shard_map/while/body/eval_jaxpr/all_gather | solution.py:126
  908.4 7.9 collective-permute-done
  916.8 18.2 %all_gather.77 = f32[8,1024]{1,0:T(8,128)S(1)} all-gather(f32[8,128]{1,0:T(8,128)S(1)} %convolution_add_fusion.12), channel_id=1, replica_groups=mesh['tm'=16,'blk'=8,'samp'=2] {'blk'}, dimensions={1}, use_global_device_ids=true | all-gather | bytes 36864 | tf_op jit(solution)/shard_map/while/body/eval_jaxpr/all_gather | solution.py:126
  936.9 7.9 collective-permute-done
  (155 shorter events, 131.3 us)
Async XLA Ops:
  6.5 51.7 %all-gather.17.cloned.1.call-start = ((), (), s32[]{:S(2)}) async-start(), calls=%async_computation.4 | async-start | bytes 2359296 | tf_op jit(solution)/shard_map/all_gather | solution.py:80
  16.1 271.2 %copy-start = (bf16[2,128,1024]{2,1,0:T(8,128)(2,1)}, bf16[2,128,1024]{2,1,0:T(8,128)(2,1)S(1)}, u32[]{:S(2)}) copy-start(bf16[2,128,1024]{2,1,0:T(8,128)(2,1)S(1)} %all_gather.63) | copy-start | bytes 1572868
  16.9 144.4 %copy-start.7 = (bf16[2,128,512]{2,1,0:T(8,128)(2,1)S(1)}, bf16[2,128,512]{2,1,0:T(8,128)(2,1)}, u32[]{:S(2)}) copy-start(bf16[2,128,512]{2,1,0:T(8,128)(2,1)} %param.22) | copy-start | bytes 786436
  16.9 123.9 %all-gather.9.cloned.1.call-start = ((), (), s32[]{:S(2)}) async-start(), calls=%async_computation | async-start | bytes 4718592 | tf_op jit(solution)/shard_map/all_gather | solution.py:101
  60.2 13.5 %copy-start.2 = (f32[128,1024]{1,0:T(8,128)}, f32[128,1024]{1,0:T(8,128)S(1)}, u32[]{:S(2)}) copy-start(f32[128,1024]{1,0:T(8,128)S(1)} %fusion.4) | copy-start | bytes 1572868
  60.3 13.5 %collective-permute-start.5 = (f32[128,1024]{1,0:T(8,128)S(1)}, f32[128,1024]{1,0:T(8,128)S(1)}, u32[]{:S(2)}, u32[]{:S(2)}) collective-permute-start(f32[128,1024]{1,0:T(8,128)S(1)} %fusion.4), channel_id=1, source_target_pairs={{0,16},{16,32},{32,48},{48,64},{64,80},{80,96},{96,112},{112,128},... | collective-permute-start | bytes 1572872 | tf_op jit(solution)/shard_map/ppermute | solution.py:25
  73.7 12.6 %collective-permute-start.7 = (f32[128,1024]{1,0:T(8,128)S(1)}, f32[128,1024]{1,0:T(8,128)S(1)}, u32[]{:S(2)}, u32[]{:S(2)}) collective-permute-start(f32[128,1024]{1,0:T(8,128)S(1)} %collective-permute-done.5), channel_id=1, source_target_pairs={{0,16},{16,32},{32,48},{48,64},{64,80},{80,96},{96,112},{112,128},... | collective-permute-start | bytes 1572872 | tf_op jit(solution)/shard_map/ppermute | solution.py:25
  86.3 0.8 copy-start.6
  87.2 128.5 %all-gather.11.cloned.1.call-start = ((), (), s32[]{:S(2)}) async-start(), calls=%async_computation.1 | async-start | bytes 4718592 | tf_op jit(solution)/shard_map/all_gather | solution.py:101
  145.4 91.9 %copy-start.8 = (f32[2,8,32]{2,1,0:T(8,128)S(1)}, f32[2,8,32]{2,1,0:T(8,128)}, u32[]{:S(2)}) copy-start(f32[2,8,32]{2,1,0:T(8,128)} %param.16) | copy-start | bytes 6148
  145.4 94.6 %copy-start.16 = (s32[16]{0:T(128)S(1)}, s32[16]{0:T(128)}, u32[]{:S(2)}) copy-start(s32[16]{0:T(128)} %param.18) | copy-start | bytes 196
  145.4 94.6 %copy-start.9 = (bf16[2,128,128]{2,1,0:T(8,128)(2,1)S(1)}, bf16[2,128,128]{2,1,0:T(8,128)(2,1)}, u32[]{:S(2)}) copy-start(bf16[2,128,128]{2,1,0:T(8,128)(2,1)} %param.21) | copy-start | bytes 196612
  145.5 100.0 %copy-start.10 = (f32[16,8,8]{0,2,1:T(8,128)S(1)}, f32[16,8,8]{0,2,1:T(8,128)}, u32[]{:S(2)}) copy-start(f32[16,8,8]{0,2,1:T(8,128)} %param.17) | copy-start | bytes 12292
  145.5 100.1 %copy-start.11 = (f32[2,8,128]{2,1,0:T(8,128)S(1)}, f32[2,8,128]{2,1,0:T(8,128)}, u32[]{:S(2)}) copy-start(f32[2,8,128]{2,1,0:T(8,128)} %param.13) | copy-start | bytes 24580
  145.5 14.8 %collective-permute-start.9 = (f32[128,1024]{1,0:T(8,128)S(1)}, f32[128,1024]{1,0:T(8,128)S(1)}, u32[]{:S(2)}, u32[]{:S(2)}) collective-permute-start(f32[128,1024]{1,0:T(8,128)S(1)} %fusion.29), channel_id=1, source_target_pairs={{0,32},{16,48},{32,64},{48,80},{64,96},{80,112},{96,128},{112,144}... | collective-permute-start | bytes 1572872 | tf_op jit(solution)/shard_map/ppermute | solution.py:25
  160.3 0.8 copy-start.5
  160.3 85.4 %copy-start.15 = (s32[2,4]{1,0:T(2,128)S(1)}, s32[2,4]{1,0:T(2,128)}, u32[]{:S(2)}) copy-start(s32[2,4]{1,0:T(2,128)} %param.15) | copy-start | bytes 100
  161.2 85.6 %copy-start.14 = (f32[2,32]{1,0:T(2,128)S(1)}, f32[2,32]{1,0:T(2,128)}, u32[]{:S(2)}) copy-start(f32[2,32]{1,0:T(2,128)} %param.14) | copy-start | bytes 772
  161.2 218.6 %all-gather.15.cloned.1.call-start = ((), (), s32[]{:S(2)}) async-start(), calls=%async_computation.3 | async-start | bytes 2359296 | tf_op jit(solution)/shard_map/all_gather | solution.py:85
  170.4 134.7 %copy-start.12 = (f32[8,128]{1,0:T(8,128)S(1)}, f32[8,128]{1,0:T(8,128)}, u32[]{:S(2)}) copy-start(f32[8,128]{1,0:T(8,128)} %param.19) | copy-start | bytes 12292
  170.5 185.3 %copy-start.13 = (f32[4,4]{1,0:T(4,128)S(1)}, f32[4,4]{1,0:T(4,128)}, u32[]{:S(2)}) copy-start(f32[4,4]{1,0:T(4,128)} %param.23) | copy-start | bytes 196
  170.5 229.5 %all-gather.13.cloned.1.call-start = ((), (), s32[]{:S(2)}) async-start(), calls=%async_computation.2 | async-start | bytes 4718592 | tf_op jit(solution)/shard_map/all_gather | solution.py:101
  220.2 16.2 %collective-permute-start.11 = (f32[128,1024]{1,0:T(8,128)S(1)}, f32[128,1024]{1,0:T(8,128)S(1)}, u32[]{:S(2)}, u32[]{:S(2)}) collective-permute-start(f32[128,1024]{1,0:T(8,128)S(1)} %fusion.30), channel_id=1, source_target_pairs={{0,64},{16,80},{32,96},{48,112},{64,128},{80,144},{96,160},{112,17... | collective-permute-start | bytes 1572872 | tf_op jit(solution)/shard_map/ppermute | solution.py:25
  236.4 0.8 copy-start.4
  237.4 8.5 collective-permute-start.1
  237.4 8.5 collective-permute-start.2
  287.5 17.6 %collective-permute-start.3 = (f32[8,128]{1,0:T(8,128)S(1)}, f32[8,128]{1,0:T(8,128)S(1)}, u32[]{:S(2)}, u32[]{:S(2)}) collective-permute-start(f32[8,128]{1,0:T(8,128)S(1)} %convolution_add_fusion.4), channel_id=1, source_target_pairs={{0,16},{16,32},{32,48},{48,64},{64,80},{80,96},{96,112},{112,128},... | collective-permute-start | bytes 12296 | tf_op jit(solution)/shard_map/ppermute | solution.py:25
  305.1 7.0 collective-permute-start.4
  330.6 4.4 collective-permute-start.6
  353.6 5.9 collective-permute-start.8
  378.2 44.9 %copy-start.1 = (bf16[2,128,1024]{2,1,0:T(8,128)(2,1)S(1)}, bf16[2,128,1024]{2,1,0:T(8,128)(2,1)}, u32[]{:S(2)}) copy-start(bf16[2,128,1024]{2,1,0:T(8,128)(2,1)} %copy-done) | copy-start | bytes 1572868
  378.3 45.1 %copy-start.3 = (f32[128,1024]{1,0:T(8,128)S(1)}, f32[128,1024]{1,0:T(8,128)}, u32[]{:S(2)}) copy-start(f32[128,1024]{1,0:T(8,128)} %copy-done.2) | copy-start | bytes 1572868
  378.3 3.5 collective-permute-start.10
  480.0 66.1 %collective-permute-start = (f32[8,1024]{1,0:T(8,128)S(1)}, f32[8,1024]{1,0:T(8,128)S(1)}, u32[]{:S(2)}, u32[]{:S(2)}) collective-permute-start(f32[8,1024]{1,0:T(8,128)S(1)} %all_gather.77), channel_id=1, source_target_pairs={{16,0},{32,16},{48,32},{64,48},{80,64},{96,80},{112,96},{128,112},... | collective-permute-start | bytes 98312 | tf_op jit(solution)/shard_map/while/body/eval_jaxpr/ppermute | solution.py:25
  564.7 9.9 %collective-permute-start = (f32[8,1024]{1,0:T(8,128)S(1)}, f32[8,1024]{1,0:T(8,128)S(1)}, u32[]{:S(2)}, u32[]{:S(2)}) collective-permute-start(f32[8,1024]{1,0:T(8,128)S(1)} %all_gather.77), channel_id=1, source_target_pairs={{16,0},{32,16},{48,32},{64,48},{80,64},{96,80},{112,96},{128,112},... | collective-permute-start | bytes 98312 | tf_op jit(solution)/shard_map/while/body/eval_jaxpr/ppermute | solution.py:25
  593.1 9.9 %collective-permute-start = (f32[8,1024]{1,0:T(8,128)S(1)}, f32[8,1024]{1,0:T(8,128)S(1)}, u32[]{:S(2)}, u32[]{:S(2)}) collective-permute-start(f32[8,1024]{1,0:T(8,128)S(1)} %all_gather.77), channel_id=1, source_target_pairs={{16,0},{32,16},{48,32},{64,48},{80,64},{96,80},{112,96},{128,112},... | collective-permute-start | bytes 98312 | tf_op jit(solution)/shard_map/while/body/eval_jaxpr/ppermute | solution.py:25
  621.6 9.9 %collective-permute-start = (f32[8,1024]{1,0:T(8,128)S(1)}, f32[8,1024]{1,0:T(8,128)S(1)}, u32[]{:S(2)}, u32[]{:S(2)}) collective-permute-start(f32[8,1024]{1,0:T(8,128)S(1)} %all_gather.77), channel_id=1, source_target_pairs={{16,0},{32,16},{48,32},{64,48},{80,64},{96,80},{112,96},{128,112},... | collective-permute-start | bytes 98312 | tf_op jit(solution)/shard_map/while/body/eval_jaxpr/ppermute | solution.py:25
  650.1 9.9 %collective-permute-start = (f32[8,1024]{1,0:T(8,128)S(1)}, f32[8,1024]{1,0:T(8,128)S(1)}, u32[]{:S(2)}, u32[]{:S(2)}) collective-permute-start(f32[8,1024]{1,0:T(8,128)S(1)} %all_gather.77), channel_id=1, source_target_pairs={{16,0},{32,16},{48,32},{64,48},{80,64},{96,80},{112,96},{128,112},... | collective-permute-start | bytes 98312 | tf_op jit(solution)/shard_map/while/body/eval_jaxpr/ppermute | solution.py:25
  678.6 9.9 %collective-permute-start = (f32[8,1024]{1,0:T(8,128)S(1)}, f32[8,1024]{1,0:T(8,128)S(1)}, u32[]{:S(2)}, u32[]{:S(2)}) collective-permute-start(f32[8,1024]{1,0:T(8,128)S(1)} %all_gather.77), channel_id=1, source_target_pairs={{16,0},{32,16},{48,32},{64,48},{80,64},{96,80},{112,96},{128,112},... | collective-permute-start | bytes 98312 | tf_op jit(solution)/shard_map/while/body/eval_jaxpr/ppermute | solution.py:25
  707.1 9.9 %collective-permute-start = (f32[8,1024]{1,0:T(8,128)S(1)}, f32[8,1024]{1,0:T(8,128)S(1)}, u32[]{:S(2)}, u32[]{:S(2)}) collective-permute-start(f32[8,1024]{1,0:T(8,128)S(1)} %all_gather.77), channel_id=1, source_target_pairs={{16,0},{32,16},{48,32},{64,48},{80,64},{96,80},{112,96},{128,112},... | collective-permute-start | bytes 98312 | tf_op jit(solution)/shard_map/while/body/eval_jaxpr/ppermute | solution.py:25
  735.6 9.9 %collective-permute-start = (f32[8,1024]{1,0:T(8,128)S(1)}, f32[8,1024]{1,0:T(8,128)S(1)}, u32[]{:S(2)}, u32[]{:S(2)}) collective-permute-start(f32[8,1024]{1,0:T(8,128)S(1)} %all_gather.77), channel_id=1, source_target_pairs={{16,0},{32,16},{48,32},{64,48},{80,64},{96,80},{112,96},{128,112},... | collective-permute-start | bytes 98312 | tf_op jit(solution)/shard_map/while/body/eval_jaxpr/ppermute | solution.py:25
  764.0 9.9 %collective-permute-start = (f32[8,1024]{1,0:T(8,128)S(1)}, f32[8,1024]{1,0:T(8,128)S(1)}, u32[]{:S(2)}, u32[]{:S(2)}) collective-permute-start(f32[8,1024]{1,0:T(8,128)S(1)} %all_gather.77), channel_id=1, source_target_pairs={{16,0},{32,16},{48,32},{64,48},{80,64},{96,80},{112,96},{128,112},... | collective-permute-start | bytes 98312 | tf_op jit(solution)/shard_map/while/body/eval_jaxpr/ppermute | solution.py:25
  792.5 9.9 %collective-permute-start = (f32[8,1024]{1,0:T(8,128)S(1)}, f32[8,1024]{1,0:T(8,128)S(1)}, u32[]{:S(2)}, u32[]{:S(2)}) collective-permute-start(f32[8,1024]{1,0:T(8,128)S(1)} %all_gather.77), channel_id=1, source_target_pairs={{16,0},{32,16},{48,32},{64,48},{80,64},{96,80},{112,96},{128,112},... | collective-permute-start | bytes 98312 | tf_op jit(solution)/shard_map/while/body/eval_jaxpr/ppermute | solution.py:25
  821.0 9.9 %collective-permute-start = (f32[8,1024]{1,0:T(8,128)S(1)}, f32[8,1024]{1,0:T(8,128)S(1)}, u32[]{:S(2)}, u32[]{:S(2)}) collective-permute-start(f32[8,1024]{1,0:T(8,128)S(1)} %all_gather.77), channel_id=1, source_target_pairs={{16,0},{32,16},{48,32},{64,48},{80,64},{96,80},{112,96},{128,112},... | collective-permute-start | bytes 98312 | tf_op jit(solution)/shard_map/while/body/eval_jaxpr/ppermute | solution.py:25
  849.5 9.9 %collective-permute-start = (f32[8,1024]{1,0:T(8,128)S(1)}, f32[8,1024]{1,0:T(8,128)S(1)}, u32[]{:S(2)}, u32[]{:S(2)}) collective-permute-start(f32[8,1024]{1,0:T(8,128)S(1)} %all_gather.77), channel_id=1, source_target_pairs={{16,0},{32,16},{48,32},{64,48},{80,64},{96,80},{112,96},{128,112},... | collective-permute-start | bytes 98312 | tf_op jit(solution)/shard_map/while/body/eval_jaxpr/ppermute | solution.py:25
  878.0 9.9 %collective-permute-start = (f32[8,1024]{1,0:T(8,128)S(1)}, f32[8,1024]{1,0:T(8,128)S(1)}, u32[]{:S(2)}, u32[]{:S(2)}) collective-permute-start(f32[8,1024]{1,0:T(8,128)S(1)} %all_gather.77), channel_id=1, source_target_pairs={{16,0},{32,16},{48,32},{64,48},{80,64},{96,80},{112,96},{128,112},... | collective-permute-start | bytes 98312 | tf_op jit(solution)/shard_map/while/body/eval_jaxpr/ppermute | solution.py:25
  906.5 9.9 %collective-permute-start = (f32[8,1024]{1,0:T(8,128)S(1)}, f32[8,1024]{1,0:T(8,128)S(1)}, u32[]{:S(2)}, u32[]{:S(2)}) collective-permute-start(f32[8,1024]{1,0:T(8,128)S(1)} %all_gather.77), channel_id=1, source_target_pairs={{16,0},{32,16},{48,32},{64,48},{80,64},{96,80},{112,96},{128,112},... | collective-permute-start | bytes 98312 | tf_op jit(solution)/shard_map/while/body/eval_jaxpr/ppermute | solution.py:25
  934.9 9.9 %collective-permute-start = (f32[8,1024]{1,0:T(8,128)S(1)}, f32[8,1024]{1,0:T(8,128)S(1)}, u32[]{:S(2)}, u32[]{:S(2)}) collective-permute-start(f32[8,1024]{1,0:T(8,128)S(1)} %all_gather.77), channel_id=1, source_target_pairs={{16,0},{32,16},{48,32},{64,48},{80,64},{96,80},{112,96},{128,112},... | collective-permute-start | bytes 98312 | tf_op jit(solution)/shard_map/while/body/eval_jaxpr/ppermute | solution.py:25
Sparse Core Ops, SparseCore 0:
  17.0 41.1 all-gather.16
  87.3 53.4 all-gather.8
  161.3 54.2 all-gather.10
  217.3 36.5 all-gather.14
  255.5 56.7 all-gather.12
where the time goes:
time: 954 us; the launch traced here: 953 us
  blocking collectives  463 us (49%)
  waiting for transfers between devices  301 us (32%)
  starting transfers between devices  137 us (14%)
  matrix products  29.7 us (3%)
  between operations  13.6 us (1%)
    all_gather x15, blocking collectives, relay_back(): complete = lax.all_gather(emitted, 'blk', axis=1, tiled=True)  273 us
    ppermute x24, waiting for transfers between devices, shifted(): lax.ppermute(value, axis, [(source, source + steps) for source in range(i...  161 us
    ppermute x24, starting transfers between devices, shifted(): lax.ppermute(value, axis, [(source, source + steps) for source in range(i...  134 us
    all_gather x3, waiting for transfers between devices, on_device(): lax.all_gather(received_m, 'blk', axis=0, tiled=True)  98.7 us
    all_gather x4, blocking collectives, on_device(): lax.all_gather(received_v, 'blk', axis=1, tiled=True)  72.5 us
    all_gather x1, waiting for transfers between devices, on_device(): lax.all_gather(trans_mats[0], 'blk', axis=0, tiled=True)  41.3 us
    all_gather x1, blocking collectives, on_device(): lax.all_gather(inputs[0], 'blk', axis=1, tiled=True)  20.3 us
    all_gather x1, blocking collectives, on_device(): all_resid = lax.all_gather(residual, 'blk', axis=2, tiled=True)  19.8 us
  transfers between devices with their start and end apart: 31, of which 26 were waited for; matrix products, arithmetic and copies ran while one was open for 1% of the time, Pallas kernels for 0%

commit v1 on v0

--- a/solution.py
+++ b/solution.py
@@ -86,7 +86,15 @@
         preferred_element_type=jnp.float32,
     )
     first_input, initial = (
-        lax.all_gather(inputs[0], "blk", axis=1, tiled=True),
+        jnp.concatenate(
+            lax.all_to_all(
+                jnp.stack([inputs[0]] * lax.psum(1, axis_name="blk"), 0),
+                axis_name="blk",
+                split_axis=0,
+                concat_axis=0,
+            ),
+            1,
+        ),
         lax.all_gather(start_mean, "blk", axis=1, tiled=True),
     )
     carry_input = apply_rows(trans_mats[1], first_input) + inputs[1]

time: 954 us -> 942 us (0.987)
    all_gather x1 -> x0, blocking collectives: 20.3 us -> none  [on_device(): lax.all_gather(inputs[0], 'blk', axis=1, tiled=True)]
    all_to_all x0 -> x1, blocking collectives: none -> 10.7 us  [on_device(): lax.all_to_all(jnp.stack([inputs[0]] * lax.psum(1, axis_name='blk'), 0),...]
where the time goes in v1:
time: 942 us; the launch traced here: 941 us
  blocking collectives  455 us (48%)
  waiting for transfers between devices  301 us (32%)
  starting transfers between devices  134 us (14%)
  matrix products  29.7 us (3%)
  between operations  13.6 us (1%)
    all_gather x15, blocking collectives, relay_back(): complete = lax.all_gather(emitted, 'blk', axis=1, tiled=True)  273 us
    ppermute x24, waiting for transfers between devices, shifted(): lax.ppermute(value, axis, [(source, source + steps) for source in range(i...  160 us
    ppermute x24, starting transfers between devices, shifted(): lax.ppermute(value, axis, [(source, source + steps) for source in range(i...  131 us
    all_gather x3, waiting for transfers between devices, on_device(): lax.all_gather(received_m, 'blk', axis=0, tiled=True)  98.7 us
    all_gather x4, blocking collectives, on_device(): lax.all_gather(received_v, 'blk', axis=1, tiled=True)  73.6 us
    all_gather x1, waiting for transfers between devices, on_device(): lax.all_gather(trans_mats[0], 'blk', axis=0, tiled=True)  41.3 us
    all_gather x1, blocking collectives, on_device(): all_resid = lax.all_gather(residual, 'blk', axis=2, tiled=True)  19.8 us
  transfers between devices with their start and end apart: 31, of which 26 were waited for; matrix products, arithmetic and copies ran while one was open for 1% of the time, Pallas kernels for 0%

profile of v1, /device:TPU:7, one launch (start us, length us, event | category | flops | bytes accessed | tf_op | source)
XLA Modules:
  0.0 940.7 jit_solution(2164384760626639911)
XLA Ops:
  6.5 9.6 %all_gather.59 = bf16[2,128,1024]{2,1,0:T(8,128)(2,1)S(1)} all-gather(bf16[2,128,512]{2,1,0:T(8,128)(2,1)} %param.20), channel_id=1, replica_groups=mesh['tm'=16,'blk'=8,'samp'=2] {'samp'}, dimensions={2}, use_global_device_ids=true | all-gather | bytes 786432 | tf_op jit(solution)/shard_map/all_gather | solution.py:46
  16.9 41.3 %all-gather.16.cloned.1.call-done = bf16[1,1024,1024]{2,1,0:T(8,128)(2,1)} async-done(((bf16[1,128,1024]{2,1,0:T(8,128)(2,1)}), bf16[1,1024,1024]{2,1,0:T(8,128)(2,1)}) %all-gather.16.cloned.1.call-update) | async-done | bytes 2097168 | tf_op jit(solution)/shard_map/all_gather | solution.py:80
  87.2 53.6 %all-gather.8.cloned.1.call-done = f32[1024,1024]{1,0:T(8,128)} async-done(((f32[128,1024]{1,0:T(8,128)}), f32[1024,1024]{1,0:T(8,128)}) %all-gather.8.cloned.1.call-update) | async-done | bytes 4194320 | tf_op jit(solution)/shard_map/all_gather | solution.py:109
  148.7 11.6 %collective-permute-done.9 = f32[128,1024]{1,0:T(8,128)S(1)} collective-permute-done((f32[128,1024]{1,0:T(8,128)S(1)}, f32[128,1024]{1,0:T(8,128)S(1)}, u32[]{:S(2)}, u32[]{:S(2)}) %collective-permute-start.9) | collective-permute-done | bytes 524320 | tf_op jit(solution)/shard_map/ppermute | solution.py:25
  161.2 8.4 all_gather.55
  170.5 45.1 %all-gather.10.cloned.1.call-done = f32[1024,1024]{1,0:T(8,128)} async-done(((f32[128,1024]{1,0:T(8,128)}), f32[1024,1024]{1,0:T(8,128)}) %all-gather.10.cloned.1.call-update) | async-done | bytes 4194320 | tf_op jit(solution)/shard_map/all_gather | solution.py:109
  224.2 12.2 %collective-permute-done.11 = f32[128,1024]{1,0:T(8,128)S(1)} collective-permute-done((f32[128,1024]{1,0:T(8,128)S(1)}, f32[128,1024]{1,0:T(8,128)S(1)}, u32[]{:S(2)}, u32[]{:S(2)}) %collective-permute-start.11) | collective-permute-done | bytes 524320 | tf_op jit(solution)/shard_map/ppermute | solution.py:25
  246.9 19.8 %all_gather.57 = f32[2,8,256]{1,0,2:T(2,128)S(1)} all-gather(f32[2,8,32]{1,0,2:T(2,128)S(1)} %copy.27), channel_id=1, replica_groups=mesh['tm'=16,'blk'=8,'samp'=2] {'blk'}, dimensions={2}, use_global_device_ids=true | all-gather | bytes 18432 | tf_op jit(solution)/shard_map/all_gather | solution.py:74
  267.0 10.7 %all_to_all.5 = f32[8,8,128]{2,1,0:T(8,128)S(1)} all-to-all(f32[8,8,128]{2,1,0:T(8,128)S(1)} %stack.21), channel_id=1, replica_groups=mesh['tm'=16,'blk'=8,'samp'=2] {'blk'}, dimensions={0} | all-to-all | bytes 65536 | tf_op jit(solution)/shard_map/all_to_all | solution.py:90
  278.0 14.3 %collective-permute-start.3 = (f32[8,128]{1,0:T(8,128)S(1)}, f32[8,128]{1,0:T(8,128)S(1)}, u32[]{:S(2)}, u32[]{:S(2)}) collective-permute-start(f32[8,128]{1,0:T(8,128)S(1)} %convolution_add_fusion.4), channel_id=1, source_target_pairs={{0,16},{16,32},{32,48},{48,64},{64,80},{80,96},{96,112},{112,128},... | collective-permute-start | bytes 12296 | tf_op jit(solution)/shard_map/ppermute | solution.py:25
  300.0 19.3 %all_gather.60 = f32[8,1024]{1,0:T(8,128)S(1)} all-gather(f32[8,128]{1,0:T(8,128)S(1)} %collective-permute-done.4), channel_id=1, replica_groups=mesh['tm'=16,'blk'=8,'samp'=2] {'blk'}, dimensions={1}, use_global_device_ids=true | all-gather | bytes 36864 | tf_op jit(solution)/shard_map/all_gather | solution.py:110
  324.2 18.1 %all_gather.62 = f32[8,1024]{1,0:T(8,128)S(1)} all-gather(f32[8,128]{1,0:T(8,128)S(1)} %collective-permute-done.6), channel_id=1, replica_groups=mesh['tm'=16,'blk'=8,'samp'=2] {'blk'}, dimensions={1}, use_global_device_ids=true | all-gather | bytes 36864 | tf_op jit(solution)/shard_map/all_gather | solution.py:110
  348.7 18.1 %all_gather.64 = f32[8,1024]{1,0:T(8,128)S(1)} all-gather(f32[8,128]{1,0:T(8,128)S(1)} %collective-permute-done.8), channel_id=1, replica_groups=mesh['tm'=16,'blk'=8,'samp'=2] {'blk'}, dimensions={1}, use_global_device_ids=true | all-gather | bytes 36864 | tf_op jit(solution)/shard_map/all_gather | solution.py:110
  370.8 18.1 %all_gather.66 = f32[8,1024]{1,0:T(8,128)S(1)} all-gather(f32[8,128]{1,0:T(8,128)S(1)} %collective-permute-done.10), channel_id=1, replica_groups=mesh['tm'=16,'blk'=8,'samp'=2] {'blk'}, dimensions={1}, use_global_device_ids=true | all-gather | bytes 36864 | tf_op jit(solution)/shard_map/all_gather | solution.py:110
  393.9 18.2 %all_gather.68 = f32[8,1024]{1,0:T(8,128)S(1)} all-gather(f32[8,128]{1,0:T(8,128)S(1)} %convolution_add_fusion.7), channel_id=1, replica_groups=mesh['tm'=16,'blk'=8,'samp'=2] {'blk'}, dimensions={1}, use_global_device_ids=true | all-gather | bytes 36864 | tf_op jit(solution)/shard_map/all_gather | solution.py:116
  413.2 18.2 %all_gather.69 = f32[2,8,1024]{2,1,0:T(8,128)S(1)} all-gather(f32[2,8,128]{2,1,0:T(8,128)S(1)} %fusion.18), channel_id=1, replica_groups=mesh['tm'=16,'blk'=8,'samp'=2] {'blk'}, dimensions={2}, use_global_device_ids=true | all-gather | bytes 73728 | tf_op jit(solution)/shard_map/all_gather | solution.py:125
  431.9 18.1 %all_gather.70 = f32[8,1024]{1,0:T(8,128)S(1)} all-gather(f32[8,128]{1,0:T(8,128)S(1)} %fusion.19), channel_id=1, replica_groups=mesh['tm'=16,'blk'=8,'samp'=2] {'blk'}, dimensions={1}, use_global_device_ids=true | all-gather | bytes 36864 | tf_op jit(solution)/shard_map/all_gather | solution.py:129
  450.2 482.5 %while.14 = (s32[]{:T(128)}, f32[8,1024]{1,0:T(8,128)S(1)}, f32[128,1024]{1,0:T(8,128)S(1)}, f32[8,128]{1,0:T(8,128)S(1)}, s32[]{:T(128)}, /*index=5*/s32[]{:T(128)}, u32[]{:T(128)}, u32[]{:T(128)}, s32[]{:T(128)}) while((s32[]{:T(128)}, f32[8,1024]{1,0:T(8,128)S(1)}, f32[128,1024]{1,0:T(8,128)S(1)}, f32[8,128]{1,0:T(8,128)S(1)}, ...), condition=%wide.region_2.3_spmd.clone, body=%wide.region_1.2_spmd.clone.sunk | while | flops 12608520 | bytes 831686 | solution.py:138
  450.8 18.2 %all_gather.73 = f32[8,1024]{1,0:T(8,128)S(1)} all-gather(f32[8,128]{1,0:T(8,128)S(1)} %convolution_add_fusion.12), channel_id=1, replica_groups=mesh['tm'=16,'blk'=8,'samp'=2] {'blk'}, dimensions={1}, use_global_device_ids=true | all-gather | bytes 36864 | tf_op jit(solution)/shard_map/while/body/eval_jaxpr/all_gather | solution.py:134
  468.9 56.4 %collective-permute-start = (f32[8,1024]{1,0:T(8,128)S(1)}, f32[8,1024]{1,0:T(8,128)S(1)}, u32[]{:S(2)}, u32[]{:S(2)}) collective-permute-start(f32[8,1024]{1,0:T(8,128)S(1)} %all_gather.73), channel_id=1, source_target_pairs={{16,0},{32,16},{48,32},{64,48},{80,64},{96,80},{112,96},{128,112},... | collective-permute-start | bytes 98312 | tf_op jit(solution)/shard_map/while/body/eval_jaxpr/ppermute | solution.py:25
  525.4 8.6 collective-permute-done
  534.4 18.2 %all_gather.73 = f32[8,1024]{1,0:T(8,128)S(1)} all-gather(f32[8,128]{1,0:T(8,128)S(1)} %convolution_add_fusion.12), channel_id=1, replica_groups=mesh['tm'=16,'blk'=8,'samp'=2] {'blk'}, dimensions={1}, use_global_device_ids=true | all-gather | bytes 36864 | tf_op jit(solution)/shard_map/while/body/eval_jaxpr/all_gather | solution.py:134
  554.5 7.9 collective-permute-done
  562.9 18.2 %all_gather.73 = f32[8,1024]{1,0:T(8,128)S(1)} all-gather(f32[8,128]{1,0:T(8,128)S(1)} %convolution_add_fusion.12), channel_id=1, replica_groups=mesh['tm'=16,'blk'=8,'samp'=2] {'blk'}, dimensions={1}, use_global_device_ids=true | all-gather | bytes 36864 | tf_op jit(solution)/shard_map/while/body/eval_jaxpr/all_gather | solution.py:134
  583.0 7.9 collective-permute-done
  591.4 18.2 %all_gather.73 = f32[8,1024]{1,0:T(8,128)S(1)} all-gather(f32[8,128]{1,0:T(8,128)S(1)} %convolution_add_fusion.12), channel_id=1, replica_groups=mesh['tm'=16,'blk'=8,'samp'=2] {'blk'}, dimensions={1}, use_global_device_ids=true | all-gather | bytes 36864 | tf_op jit(solution)/shard_map/while/body/eval_jaxpr/all_gather | solution.py:134
  611.5 7.9 collective-permute-done
  619.9 18.2 %all_gather.73 = f32[8,1024]{1,0:T(8,128)S(1)} all-gather(f32[8,128]{1,0:T(8,128)S(1)} %convolution_add_fusion.12), channel_id=1, replica_groups=mesh['tm'=16,'blk'=8,'samp'=2] {'blk'}, dimensions={1}, use_global_device_ids=true | all-gather | bytes 36864 | tf_op jit(solution)/shard_map/while/body/eval_jaxpr/all_gather | solution.py:134
  640.0 7.9 collective-permute-done
  648.3 18.2 %all_gather.73 = f32[8,1024]{1,0:T(8,128)S(1)} all-gather(f32[8,128]{1,0:T(8,128)S(1)} %convolution_add_fusion.12), channel_id=1, replica_groups=mesh['tm'=16,'blk'=8,'samp'=2] {'blk'}, dimensions={1}, use_global_device_ids=true | all-gather | bytes 36864 | tf_op jit(solution)/shard_map/while/body/eval_jaxpr/all_gather | solution.py:134
  676.8 18.2 %all_gather.73 = f32[8,1024]{1,0:T(8,128)S(1)} all-gather(f32[8,128]{1,0:T(8,128)S(1)} %convolution_add_fusion.12), channel_id=1, replica_groups=mesh['tm'=16,'blk'=8,'samp'=2] {'blk'}, dimensions={1}, use_global_device_ids=true | all-gather | bytes 36864 | tf_op jit(solution)/shard_map/while/body/eval_jaxpr/all_gather | solution.py:134
  696.9 7.9 collective-permute-done
  705.3 18.2 %all_gather.73 = f32[8,1024]{1,0:T(8,128)S(1)} all-gather(f32[8,128]{1,0:T(8,128)S(1)} %convolution_add_fusion.12), channel_id=1, replica_groups=mesh['tm'=16,'blk'=8,'samp'=2] {'blk'}, dimensions={1}, use_global_device_ids=true | all-gather | bytes 36864 | tf_op jit(solution)/shard_map/while/body/eval_jaxpr/all_gather | solution.py:134
  725.4 7.9 collective-permute-done
  733.8 18.2 %all_gather.73 = f32[8,1024]{1,0:T(8,128)S(1)} all-gather(f32[8,128]{1,0:T(8,128)S(1)} %convolution_add_fusion.12), channel_id=1, replica_groups=mesh['tm'=16,'blk'=8,'samp'=2] {'blk'}, dimensions={1}, use_global_device_ids=true | all-gather | bytes 36864 | tf_op jit(solution)/shard_map/while/body/eval_jaxpr/all_gather | solution.py:134
  753.9 7.9 collective-permute-done
  762.3 18.2 %all_gather.73 = f32[8,1024]{1,0:T(8,128)S(1)} all-gather(f32[8,128]{1,0:T(8,128)S(1)} %convolution_add_fusion.12), channel_id=1, replica_groups=mesh['tm'=16,'blk'=8,'samp'=2] {'blk'}, dimensions={1}, use_global_device_ids=true | all-gather | bytes 36864 | tf_op jit(solution)/shard_map/while/body/eval_jaxpr/all_gather | solution.py:134
  782.4 7.9 collective-permute-done
  790.8 18.2 %all_gather.73 = f32[8,1024]{1,0:T(8,128)S(1)} all-gather(f32[8,128]{1,0:T(8,128)S(1)} %convolution_add_fusion.12), channel_id=1, replica_groups=mesh['tm'=16,'blk'=8,'samp'=2] {'blk'}, dimensions={1}, use_global_device_ids=true | all-gather | bytes 36864 | tf_op jit(solution)/shard_map/while/body/eval_jaxpr/all_gather | solution.py:134
  810.9 7.9 collective-permute-done
  819.2 18.2 %all_gather.73 = f32[8,1024]{1,0:T(8,128)S(1)} all-gather(f32[8,128]{1,0:T(8,128)S(1)} %convolution_add_fusion.12), channel_id=1, replica_groups=mesh['tm'=16,'blk'=8,'samp'=2] {'blk'}, dimensions={1}, use_global_device_ids=true | all-gather | bytes 36864 | tf_op jit(solution)/shard_map/while/body/eval_jaxpr/all_gather | solution.py:134
  839.4 7.9 collective-permute-done
  847.7 18.2 %all_gather.73 = f32[8,1024]{1,0:T(8,128)S(1)} all-gather(f32[8,128]{1,0:T(8,128)S(1)} %convolution_add_fusion.12), channel_id=1, replica_groups=mesh['tm'=16,'blk'=8,'samp'=2] {'blk'}, dimensions={1}, use_global_device_ids=true | all-gather | bytes 36864 | tf_op jit(solution)/shard_map/while/body/eval_jaxpr/all_gather | solution.py:134
  867.8 7.9 collective-permute-done
  876.2 18.2 %all_gather.73 = f32[8,1024]{1,0:T(8,128)S(1)} all-gather(f32[8,128]{1,0:T(8,128)S(1)} %convolution_add_fusion.12), channel_id=1, replica_groups=mesh['tm'=16,'blk'=8,'samp'=2] {'blk'}, dimensions={1}, use_global_device_ids=true | all-gather | bytes 36864 | tf_op jit(solution)/shard_map/while/body/eval_jaxpr/all_gather | solution.py:134
  896.3 7.9 collective-permute-done
  904.7 18.2 %all_gather.73 = f32[8,1024]{1,0:T(8,128)S(1)} all-gather(f32[8,128]{1,0:T(8,128)S(1)} %convolution_add_fusion.12), channel_id=1, replica_groups=mesh['tm'=16,'blk'=8,'samp'=2] {'blk'}, dimensions={1}, use_global_device_ids=true | all-gather | bytes 36864 | tf_op jit(solution)/shard_map/while/body/eval_jaxpr/all_gather | solution.py:134
  924.8 7.9 collective-permute-done
  (156 shorter events, 131.3 us)
Async XLA Ops:
  6.5 51.7 %all-gather.16.cloned.1.call-start = ((), (), s32[]{:S(2)}) async-start(), calls=%async_computation.5 | async-start | bytes 2359296 | tf_op jit(solution)/shard_map/all_gather | solution.py:80
  16.1 261.7 %copy-start = (bf16[2,128,1024]{2,1,0:T(8,128)(2,1)}, bf16[2,128,1024]{2,1,0:T(8,128)(2,1)S(1)}, u32[]{:S(2)}) copy-start(bf16[2,128,1024]{2,1,0:T(8,128)(2,1)S(1)} %all_gather.59) | copy-start | bytes 1572868
  16.9 144.4 %copy-start.7 = (bf16[2,128,512]{2,1,0:T(8,128)(2,1)S(1)}, bf16[2,128,512]{2,1,0:T(8,128)(2,1)}, u32[]{:S(2)}) copy-start(bf16[2,128,512]{2,1,0:T(8,128)(2,1)} %param.22) | copy-start | bytes 786436
  16.9 123.9 %all-gather.8.cloned.1.call-start = ((), (), s32[]{:S(2)}) async-start(), calls=%async_computation.1 | async-start | bytes 4718592 | tf_op jit(solution)/shard_map/all_gather | solution.py:109
  60.2 13.5 %copy-start.2 = (f32[128,1024]{1,0:T(8,128)}, f32[128,1024]{1,0:T(8,128)S(1)}, u32[]{:S(2)}) copy-start(f32[128,1024]{1,0:T(8,128)S(1)} %fusion.4) | copy-start | bytes 1572868
  60.3 13.5 %collective-permute-start.5 = (f32[128,1024]{1,0:T(8,128)S(1)}, f32[128,1024]{1,0:T(8,128)S(1)}, u32[]{:S(2)}, u32[]{:S(2)}) collective-permute-start(f32[128,1024]{1,0:T(8,128)S(1)} %fusion.4), channel_id=1, source_target_pairs={{0,16},{16,32},{32,48},{48,64},{64,80},{80,96},{96,112},{112,128},... | collective-permute-start | bytes 1572872 | tf_op jit(solution)/shard_map/ppermute | solution.py:25
  73.7 12.6 %collective-permute-start.7 = (f32[128,1024]{1,0:T(8,128)S(1)}, f32[128,1024]{1,0:T(8,128)S(1)}, u32[]{:S(2)}, u32[]{:S(2)}) collective-permute-start(f32[128,1024]{1,0:T(8,128)S(1)} %collective-permute-done.5), channel_id=1, source_target_pairs={{0,16},{16,32},{32,48},{48,64},{64,80},{80,96},{96,112},{112,128},... | collective-permute-start | bytes 1572872 | tf_op jit(solution)/shard_map/ppermute | solution.py:25
  86.3 0.8 copy-start.6
  87.2 128.5 %all-gather.10.cloned.1.call-start = ((), (), s32[]{:S(2)}) async-start(), calls=%async_computation.2 | async-start | bytes 4718592 | tf_op jit(solution)/shard_map/all_gather | solution.py:109
  145.4 91.9 %copy-start.8 = (f32[2,8,32]{2,1,0:T(8,128)S(1)}, f32[2,8,32]{2,1,0:T(8,128)}, u32[]{:S(2)}) copy-start(f32[2,8,32]{2,1,0:T(8,128)} %param.16) | copy-start | bytes 6148
  145.4 94.6 %copy-start.16 = (s32[16]{0:T(128)S(1)}, s32[16]{0:T(128)}, u32[]{:S(2)}) copy-start(s32[16]{0:T(128)} %param.18) | copy-start | bytes 196
  145.4 94.6 %copy-start.9 = (bf16[2,128,128]{2,1,0:T(8,128)(2,1)S(1)}, bf16[2,128,128]{2,1,0:T(8,128)(2,1)}, u32[]{:S(2)}) copy-start(bf16[2,128,128]{2,1,0:T(8,128)(2,1)} %param.21) | copy-start | bytes 196612
  145.5 100.0 %copy-start.10 = (f32[16,8,8]{0,2,1:T(8,128)S(1)}, f32[16,8,8]{0,2,1:T(8,128)}, u32[]{:S(2)}) copy-start(f32[16,8,8]{0,2,1:T(8,128)} %param.17) | copy-start | bytes 12292
  145.5 100.1 %copy-start.11 = (f32[2,8,128]{2,1,0:T(8,128)S(1)}, f32[2,8,128]{2,1,0:T(8,128)}, u32[]{:S(2)}) copy-start(f32[2,8,128]{2,1,0:T(8,128)} %param.13) | copy-start | bytes 24580
  145.5 14.8 %collective-permute-start.9 = (f32[128,1024]{1,0:T(8,128)S(1)}, f32[128,1024]{1,0:T(8,128)S(1)}, u32[]{:S(2)}, u32[]{:S(2)}) collective-permute-start(f32[128,1024]{1,0:T(8,128)S(1)} %fusion.29), channel_id=1, source_target_pairs={{0,32},{16,48},{32,64},{48,80},{64,96},{80,112},{96,128},{112,144}... | collective-permute-start | bytes 1572872 | tf_op jit(solution)/shard_map/ppermute | solution.py:25
  160.3 0.8 copy-start.5
  160.3 85.4 %copy-start.15 = (s32[2,4]{1,0:T(2,128)S(1)}, s32[2,4]{1,0:T(2,128)}, u32[]{:S(2)}) copy-start(s32[2,4]{1,0:T(2,128)} %param.15) | copy-start | bytes 100
  161.2 85.6 %copy-start.14 = (f32[2,32]{1,0:T(2,128)S(1)}, f32[2,32]{1,0:T(2,128)}, u32[]{:S(2)}) copy-start(f32[2,32]{1,0:T(2,128)} %param.14) | copy-start | bytes 772
  161.2 207.6 %all-gather.14.cloned.1.call-start = ((), (), s32[]{:S(2)}) async-start(), calls=%async_computation.4 | async-start | bytes 2359296 | tf_op jit(solution)/shard_map/all_gather | solution.py:85
  170.4 122.6 %copy-start.12 = (f32[8,128]{1,0:T(8,128)S(1)}, f32[8,128]{1,0:T(8,128)}, u32[]{:S(2)}) copy-start(f32[8,128]{1,0:T(8,128)} %param.19) | copy-start | bytes 12292
  170.5 174.9 %copy-start.13 = (f32[4,4]{1,0:T(4,128)S(1)}, f32[4,4]{1,0:T(4,128)}, u32[]{:S(2)}) copy-start(f32[4,4]{1,0:T(4,128)} %param.23) | copy-start | bytes 196
  170.5 218.5 %all-gather.12.cloned.1.call-start = ((), (), s32[]{:S(2)}) async-start(), calls=%async_computation.3 | async-start | bytes 4718592 | tf_op jit(solution)/shard_map/all_gather | solution.py:109
  220.2 16.2 %collective-permute-start.11 = (f32[128,1024]{1,0:T(8,128)S(1)}, f32[128,1024]{1,0:T(8,128)S(1)}, u32[]{:S(2)}, u32[]{:S(2)}) collective-permute-start(f32[128,1024]{1,0:T(8,128)S(1)} %fusion.30), channel_id=1, source_target_pairs={{0,64},{16,80},{32,96},{48,112},{64,128},{80,144},{96,160},{112,17... | collective-permute-start | bytes 1572872 | tf_op jit(solution)/shard_map/ppermute | solution.py:25
  236.4 0.8 copy-start.4
  237.4 8.5 collective-permute-start.1
  237.4 8.5 collective-permute-start.2
  278.0 15.0 %collective-permute-start.3 = (f32[8,128]{1,0:T(8,128)S(1)}, f32[8,128]{1,0:T(8,128)S(1)}, u32[]{:S(2)}, u32[]{:S(2)}) collective-permute-start(f32[8,128]{1,0:T(8,128)S(1)} %convolution_add_fusion.4), channel_id=1, source_target_pairs={{0,16},{16,32},{32,48},{48,64},{64,80},{80,96},{96,112},{112,128},... | collective-permute-start | bytes 12296 | tf_op jit(solution)/shard_map/ppermute | solution.py:25
  293.0 7.0 collective-permute-start.4
  319.8 4.4 collective-permute-start.6
  342.7 5.9 collective-permute-start.8
  367.2 44.9 %copy-start.1 = (bf16[2,128,1024]{2,1,0:T(8,128)(2,1)S(1)}, bf16[2,128,1024]{2,1,0:T(8,128)(2,1)}, u32[]{:S(2)}) copy-start(bf16[2,128,1024]{2,1,0:T(8,128)(2,1)} %copy-done) | copy-start | bytes 1572868
  367.3 45.1 %copy-start.3 = (f32[128,1024]{1,0:T(8,128)S(1)}, f32[128,1024]{1,0:T(8,128)}, u32[]{:S(2)}) copy-start(f32[128,1024]{1,0:T(8,128)} %copy-done.2) | copy-start | bytes 1572868
  367.3 3.5 collective-permute-start.10
  468.9 65.0 %collective-permute-start = (f32[8,1024]{1,0:T(8,128)S(1)}, f32[8,1024]{1,0:T(8,128)S(1)}, u32[]{:S(2)}, u32[]{:S(2)}) collective-permute-start(f32[8,1024]{1,0:T(8,128)S(1)} %all_gather.73), channel_id=1, source_target_pairs={{16,0},{32,16},{48,32},{64,48},{80,64},{96,80},{112,96},{128,112},... | collective-permute-start | bytes 98312 | tf_op jit(solution)/shard_map/while/body/eval_jaxpr/ppermute | solution.py:25
  552.6 9.9 %collective-permute-start = (f32[8,1024]{1,0:T(8,128)S(1)}, f32[8,1024]{1,0:T(8,128)S(1)}, u32[]{:S(2)}, u32[]{:S(2)}) collective-permute-start(f32[8,1024]{1,0:T(8,128)S(1)} %all_gather.73), channel_id=1, source_target_pairs={{16,0},{32,16},{48,32},{64,48},{80,64},{96,80},{112,96},{128,112},... | collective-permute-start | bytes 98312 | tf_op jit(solution)/shard_map/while/body/eval_jaxpr/ppermute | solution.py:25
  581.1 9.9 %collective-permute-start = (f32[8,1024]{1,0:T(8,128)S(1)}, f32[8,1024]{1,0:T(8,128)S(1)}, u32[]{:S(2)}, u32[]{:S(2)}) collective-permute-start(f32[8,1024]{1,0:T(8,128)S(1)} %all_gather.73), channel_id=1, source_target_pairs={{16,0},{32,16},{48,32},{64,48},{80,64},{96,80},{112,96},{128,112},... | collective-permute-start | bytes 98312 | tf_op jit(solution)/shard_map/while/body/eval_jaxpr/ppermute | solution.py:25
  609.6 9.9 %collective-permute-start = (f32[8,1024]{1,0:T(8,128)S(1)}, f32[8,1024]{1,0:T(8,128)S(1)}, u32[]{:S(2)}, u32[]{:S(2)}) collective-permute-start(f32[8,1024]{1,0:T(8,128)S(1)} %all_gather.73), channel_id=1, source_target_pairs={{16,0},{32,16},{48,32},{64,48},{80,64},{96,80},{112,96},{128,112},... | collective-permute-start | bytes 98312 | tf_op jit(solution)/shard_map/while/body/eval_jaxpr/ppermute | solution.py:25
  638.0 9.9 %collective-permute-start = (f32[8,1024]{1,0:T(8,128)S(1)}, f32[8,1024]{1,0:T(8,128)S(1)}, u32[]{:S(2)}, u32[]{:S(2)}) collective-permute-start(f32[8,1024]{1,0:T(8,128)S(1)} %all_gather.73), channel_id=1, source_target_pairs={{16,0},{32,16},{48,32},{64,48},{80,64},{96,80},{112,96},{128,112},... | collective-permute-start | bytes 98312 | tf_op jit(solution)/shard_map/while/body/eval_jaxpr/ppermute | solution.py:25
  666.5 9.9 %collective-permute-start = (f32[8,1024]{1,0:T(8,128)S(1)}, f32[8,1024]{1,0:T(8,128)S(1)}, u32[]{:S(2)}, u32[]{:S(2)}) collective-permute-start(f32[8,1024]{1,0:T(8,128)S(1)} %all_gather.73), channel_id=1, source_target_pairs={{16,0},{32,16},{48,32},{64,48},{80,64},{96,80},{112,96},{128,112},... | collective-permute-start | bytes 98312 | tf_op jit(solution)/shard_map/while/body/eval_jaxpr/ppermute | solution.py:25
  695.0 9.9 %collective-permute-start = (f32[8,1024]{1,0:T(8,128)S(1)}, f32[8,1024]{1,0:T(8,128)S(1)}, u32[]{:S(2)}, u32[]{:S(2)}) collective-permute-start(f32[8,1024]{1,0:T(8,128)S(1)} %all_gather.73), channel_id=1, source_target_pairs={{16,0},{32,16},{48,32},{64,48},{80,64},{96,80},{112,96},{128,112},... | collective-permute-start | bytes 98312 | tf_op jit(solution)/shard_map/while/body/eval_jaxpr/ppermute | solution.py:25
  723.5 9.9 %collective-permute-start = (f32[8,1024]{1,0:T(8,128)S(1)}, f32[8,1024]{1,0:T(8,128)S(1)}, u32[]{:S(2)}, u32[]{:S(2)}) collective-permute-start(f32[8,1024]{1,0:T(8,128)S(1)} %all_gather.73), channel_id=1, source_target_pairs={{16,0},{32,16},{48,32},{64,48},{80,64},{96,80},{112,96},{128,112},... | collective-permute-start | bytes 98312 | tf_op jit(solution)/shard_map/while/body/eval_jaxpr/ppermute | solution.py:25
  752.0 9.9 %collective-permute-start = (f32[8,1024]{1,0:T(8,128)S(1)}, f32[8,1024]{1,0:T(8,128)S(1)}, u32[]{:S(2)}, u32[]{:S(2)}) collective-permute-start(f32[8,1024]{1,0:T(8,128)S(1)} %all_gather.73), channel_id=1, source_target_pairs={{16,0},{32,16},{48,32},{64,48},{80,64},{96,80},{112,96},{128,112},... | collective-permute-start | bytes 98312 | tf_op jit(solution)/shard_map/while/body/eval_jaxpr/ppermute | solution.py:25
  780.5 9.9 %collective-permute-start = (f32[8,1024]{1,0:T(8,128)S(1)}, f32[8,1024]{1,0:T(8,128)S(1)}, u32[]{:S(2)}, u32[]{:S(2)}) collective-permute-start(f32[8,1024]{1,0:T(8,128)S(1)} %all_gather.73), channel_id=1, source_target_pairs={{16,0},{32,16},{48,32},{64,48},{80,64},{96,80},{112,96},{128,112},... | collective-permute-start | bytes 98312 | tf_op jit(solution)/shard_map/while/body/eval_jaxpr/ppermute | solution.py:25
  808.9 9.9 %collective-permute-start = (f32[8,1024]{1,0:T(8,128)S(1)}, f32[8,1024]{1,0:T(8,128)S(1)}, u32[]{:S(2)}, u32[]{:S(2)}) collective-permute-start(f32[8,1024]{1,0:T(8,128)S(1)} %all_gather.73), channel_id=1, source_target_pairs={{16,0},{32,16},{48,32},{64,48},{80,64},{96,80},{112,96},{128,112},... | collective-permute-start | bytes 98312 | tf_op jit(solution)/shard_map/while/body/eval_jaxpr/ppermute | solution.py:25
  837.4 9.9 %collective-permute-start = (f32[8,1024]{1,0:T(8,128)S(1)}, f32[8,1024]{1,0:T(8,128)S(1)}, u32[]{:S(2)}, u32[]{:S(2)}) collective-permute-start(f32[8,1024]{1,0:T(8,128)S(1)} %all_gather.73), channel_id=1, source_target_pairs={{16,0},{32,16},{48,32},{64,48},{80,64},{96,80},{112,96},{128,112},... | collective-permute-start | bytes 98312 | tf_op jit(solution)/shard_map/while/body/eval_jaxpr/ppermute | solution.py:25
  865.9 9.9 %collective-permute-start = (f32[8,1024]{1,0:T(8,128)S(1)}, f32[8,1024]{1,0:T(8,128)S(1)}, u32[]{:S(2)}, u32[]{:S(2)}) collective-permute-start(f32[8,1024]{1,0:T(8,128)S(1)} %all_gather.73), channel_id=1, source_target_pairs={{16,0},{32,16},{48,32},{64,48},{80,64},{96,80},{112,96},{128,112},... | collective-permute-start | bytes 98312 | tf_op jit(solution)/shard_map/while/body/eval_jaxpr/ppermute | solution.py:25
  894.4 9.9 %collective-permute-start = (f32[8,1024]{1,0:T(8,128)S(1)}, f32[8,1024]{1,0:T(8,128)S(1)}, u32[]{:S(2)}, u32[]{:S(2)}) collective-permute-start(f32[8,1024]{1,0:T(8,128)S(1)} %all_gather.73), channel_id=1, source_target_pairs={{16,0},{32,16},{48,32},{64,48},{80,64},{96,80},{112,96},{128,112},... | collective-permute-start | bytes 98312 | tf_op jit(solution)/shard_map/while/body/eval_jaxpr/ppermute | solution.py:25
  922.9 9.9 %collective-permute-start = (f32[8,1024]{1,0:T(8,128)S(1)}, f32[8,1024]{1,0:T(8,128)S(1)}, u32[]{:S(2)}, u32[]{:S(2)}) collective-permute-start(f32[8,1024]{1,0:T(8,128)S(1)} %all_gather.73), channel_id=1, source_target_pairs={{16,0},{32,16},{48,32},{64,48},{80,64},{96,80},{112,96},{128,112},... | collective-permute-start | bytes 98312 | tf_op jit(solution)/shard_map/while/body/eval_jaxpr/ppermute | solution.py:25
Sparse Core Ops, SparseCore 0:
  17.0 41.1 all-gather.15
  87.3 53.4 all-gather.7
  161.3 54.2 all-gather.9
  217.3 36.5 all-gather.13
  255.5 57.3 all-gather.11
